TPU v7x, 128 devices: a whole 4x4x4 slice. The times are simulated.
128 devices in a mesh: dp: 16 (over y, x), row: 4 (over z), col: 2 (over core).
Axes of the slice: x: 4, y: 4, z: 4, core: 2. Of those that a mesh axis runs over, the one named last changes fastest.
Arguments:
- tokens: bfloat16 [4096, 4096], P(('dp', 'col'), 'row'), may hold values from -6 to 6
- w_up: bfloat16 [4096, 16384], P('row', 'col'), may hold values from -0.09375 to 0.09375
- w_down: bfloat16 [4096, 16384], P('row', 'col'), may hold values from -0.046875 to 0.046875
- cotangent: bfloat16 [4096, 4096], P(('dp', 'col'), 'row'), may hold values from -6 to 6
Outputs:
- output: bfloat16 [4096, 4096], P(('dp', 'col'), 'row')
- input_grad: bfloat16 [4096, 4096], P(('dp', 'col'), 'row')
- up_grad: float32 [4096, 16384], P('row', ('col', 'dp'))
- down_grad: float32 [4096, 16384], P('row', ('col', 'dp'))
All inputs are finite; a program needn't handle non-finite values.
Results may differ from a plain program's by a relative error of at most 0.018.
Values may be sent and summed in bfloat16 or wider, within the bound.
A program may use at most 192 MiB of HBM per device.

v0:
```python
import jax
import jax.numpy as jnp
from jax import lax
from jax.sharding import PartitionSpec as P

gelu_coef = 0.7978845608
cubic_coef = 0.044715


def rounded(matrix):
    return lax.optimization_barrier(matrix.astype(jnp.bfloat16)).astype(jnp.float32)


def gelu_pair(hidden):
    tangent = jnp.tanh(gelu_coef * (hidden + cubic_coef * hidden * hidden * hidden))
    activated = 0.5 * hidden * (1.0 + tangent)
    derivative = 0.5 * (1.0 + tangent) + 0.5 * hidden * (1.0 - tangent * tangent) * gelu_coef * (
        1.0 + 3.0 * cubic_coef * hidden * hidden
    )
    return (activated, derivative)


def times_transposed(left, right):
    return lax.dot_general(
        left, right, (((1,), (1,)), ((), ())), preferred_element_type=jnp.float32
    )


def over_tokens(left, right):
    return lax.dot_general(
        left, right, (((0,), (0,)), ((), ())), preferred_element_type=jnp.float32
    )


def body(tokens, w_up, w_down, cotangent):
    batch_total = tokens.shape[0] * lax.axis_size("col") * lax.axis_size("dp")
    grad_scale = float(batch_total) ** (-0.5)
    token_block = lax.all_gather(tokens, "col", axis=0, tiled=True)
    picked = token_block
    hidden = lax.psum_scatter(
        rounded(jnp.dot(picked, w_up, preferred_element_type=jnp.float32)).astype(jnp.bfloat16),
        "row",
        scatter_dimension=0,
        tiled=True,
    ).astype(jnp.float32)
    activated, derivative = gelu_pair(hidden)
    act_all = lax.all_gather(activated.astype(jnp.bfloat16), "row", axis=0, tiled=True)
    picked = act_all
    output = lax.psum_scatter(
        times_transposed(picked, w_down).astype(jnp.bfloat16),
        "col",
        scatter_dimension=0,
        tiled=True,
    )
    grad_block = lax.all_gather(cotangent, "col", axis=0, tiled=True)
    picked = grad_block
    back = lax.psum_scatter(
        rounded(jnp.dot(picked, w_down, preferred_element_type=jnp.float32)).astype(jnp.bfloat16),
        "row",
        scatter_dimension=0,
        tiled=True,
    ).astype(jnp.float32)
    grad_all = lax.all_gather((back * derivative).astype(jnp.bfloat16), "row", axis=0, tiled=True)
    picked = grad_all
    input_grad = lax.psum_scatter(
        times_transposed(picked, w_up).astype(jnp.bfloat16), "col", scatter_dimension=0, tiled=True
    )
    up_local = grad_scale * over_tokens(token_block, grad_all)
    down_local = grad_scale * over_tokens(grad_block, act_all)
    up_grad, down_grad = (
        lax.psum_scatter(
            up_local.astype(jnp.bfloat16), "dp", scatter_dimension=1, tiled=True
        ).astype(jnp.float32),
        lax.psum_scatter(
            down_local.astype(jnp.bfloat16), "dp", scatter_dimension=1, tiled=True
        ).astype(jnp.float32),
    )
    return (output, input_grad, up_grad, down_grad)


def solution(mesh):
    placed = (P(("dp", "col"), "row"), P("row", "col"), P("row", "col"), P(("dp", "col"), "row"))
    return jax.shard_map(
        body,
        mesh=mesh,
        in_specs=placed,
        out_specs=(
            P(("dp", "col"), "row"),
            P(("dp", "col"), "row"),
            P("row", ("col", "dp")),
            P("row", ("col", "dp")),
        ),
        check_vma=False,
    )
```

profile of v0, /device:TPU:1, one launch (start us, length us, event | category | flops | bytes accessed | tf_op | source)
XLA Modules:
  0.0 486.7 jit_solution(16878680931594667336)
XLA Ops:
  7.2 0.0 reduce-scatter.11.cloned.1.call-start
  7.2 3.4 all_gather.14
  10.6 11.8 %convolution_convert_fusion = bf16[256,8192]{1,0:T(8,128)(2,1)} fusion(bf16[256,1024]{1,0:T(8,128)(2,1)S(1)} %all_gather.14, bf16[1024,8192]{1,0:T(8,128)(2,1)} %param.6), kind=kOutput, calls=%fused_computation.4 | convolution fusion | flops 4297064448 | bytes 21495808 | tf_op jit(solution)/shard_map/dot_general | solution.py:58
  22.4 0.0 copy-start
  22.4 0.0 reduce-scatter.11.cloned.1.call-update
  22.4 0.0 reduce-scatter.7.cloned.1.call-start
  22.5 0.9 copy-done
  23.4 2.2 all_gather.12
  25.5 11.8 %convolution_convert_fusion.1 = bf16[256,8192]{1,0:T(8,128)(2,1)} fusion(bf16[256,1024]{1,0:T(8,128)(2,1)S(1)} %all_gather.12, bf16[1024,8192]{1,0:T(8,128)(2,1)} %param.5), kind=kOutput, calls=%fused_computation.5 | convolution fusion | flops 4297064448 | bytes 21495808 | tf_op jit(solution)/shard_map/dot_general | solution.py:41
  37.4 0.0 reduce-scatter.7.cloned.1.call-update
  37.4 0.0 all-gather.5.cloned.1.call-start
  37.5 34.3 %reduce-scatter.11.cloned.1.call-done = bf16[64,8192]{1,0:T(8,128)(2,1)} async-done(((bf16[256,8192]{1,0:T(8,128)(2,1)}), bf16[64,8192]{1,0:T(8,128)(2,1)}) %reduce-scatter.11.cloned.1.call-update) | async-done | bytes 1048592 | tf_op jit(solution)/shard_map/reduce_scatter | solution.py:57
  71.8 49.1 %reduce-scatter.7.cloned.1.call-done = bf16[64,8192]{1,0:T(8,128)(2,1)} async-done(((bf16[256,8192]{1,0:T(8,128)(2,1)}), bf16[64,8192]{1,0:T(8,128)(2,1)}) %reduce-scatter.7.cloned.1.call-update) | async-done | bytes 1048592 | tf_op jit(solution)/shard_map/reduce_scatter | solution.py:40
  120.9 4.4 fusion.9
  125.3 0.0 all-gather.5.cloned.1.call-update
  125.3 0.0 all-gather.3.cloned.1.call-start
  125.3 0.5 all-gather.3.cloned.1.call-update
  125.9 0.0 reduce-scatter.15.cloned.1.call-start
  125.9 47.4 %all-gather.5.cloned.1.call-done = bf16[256,8192]{1,0:T(8,128)(2,1)} async-done(((bf16[64,8192]{1,0:T(8,128)(2,1)}), bf16[256,8192]{1,0:T(8,128)(2,1)}) %all-gather.5.cloned.1.call-update) | async-done | bytes 4194320 | tf_op jit(solution)/shard_map/all_gather | solution.py:63
  173.4 10.5 %fusion = bf16[1024,8192]{0,1:T(8,128)(2,1)} fusion(bf16[256,8192]{1,0:T(8,128)(2,1)} %all-gather.5.cloned.1.call-done, bf16[256,1024]{1,0:T(8,128)(2,1)S(1)} %all_gather.12), kind=kOutput, calls=%fused_computation.2 | convolution fusion | flops 4311744512 | bytes 21495808 | tf_op jit(solution)/shard_map/dot_general | solution.py:30
  183.8 0.0 reduce-scatter.15.cloned.1.call-update
  183.8 0.0 reduce-scatter.17.cloned.1.call-start
  183.9 40.2 %all-gather.3.cloned.1.call-done = bf16[256,8192]{1,0:T(8,128)(2,1)} async-done(((bf16[64,8192]{1,0:T(8,128)(2,1)}), bf16[256,8192]{1,0:T(8,128)(2,1)}) %all-gather.3.cloned.1.call-update) | async-done | bytes 4194320 | tf_op jit(solution)/shard_map/all_gather | solution.py:47
  224.1 10.5 %fusion.1 = bf16[1024,8192]{0,1:T(8,128)(2,1)} fusion(bf16[256,8192]{1,0:T(8,128)(2,1)} %all-gather.3.cloned.1.call-done, bf16[256,1024]{1,0:T(8,128)(2,1)S(1)} %all_gather.14), kind=kOutput, calls=%fused_computation.3 | convolution fusion | flops 4311744512 | bytes 21495808 | tf_op jit(solution)/shard_map/dot_general | solution.py:30
  234.6 0.0 reduce-scatter.17.cloned.1.call-update
  234.6 0.2 reduce-scatter.9.cloned.1.call-start
  234.8 13.2 %convolution_convert_fusion.3 = bf16[256,1024]{1,0:T(8,128)(2,1)} fusion(bf16[256,8192]{1,0:T(8,128)(2,1)} %all-gather.3.cloned.1.call-done, bf16[1024,8192]{1,0:T(8,128)(2,1)} %param.6), kind=kOutput, calls=%fused_computation.25 | convolution fusion | flops 4295229440 | bytes 21495808 | tf_op jit(solution)/shard_map/dot_general | solution.py:24
  248.0 0.0 reduce-scatter.9.cloned.1.call-update
  248.0 0.0 reduce-scatter.13.cloned.1.call-start
  248.1 12.9 %convolution_convert_fusion.2 = bf16[256,1024]{1,0:T(8,128)(2,1)} fusion(bf16[256,8192]{1,0:T(8,128)(2,1)} %all-gather.5.cloned.1.call-done, bf16[1024,8192]{1,0:T(8,128)(2,1)} %param.5), kind=kOutput, calls=%fused_computation.24 | convolution fusion | flops 4295229440 | bytes 21495808 | tf_op jit(solution)/shard_map/dot_general | solution.py:24
  260.9 0.0 reduce-scatter.13.cloned.1.call-update
  261.0 76.7 %reduce-scatter.15.cloned.1.call-done = bf16[1024,512]{0,1:T(8,128)(2,1)} async-done(((bf16[1024,8192]{0,1:T(8,128)(2,1)}), bf16[1024,512]{0,1:T(8,128)(2,1)}) %reduce-scatter.15.cloned.1.call-update) | async-done | bytes 1048592 | tf_op jit(solution)/shard_map/reduce_scatter | solution.py:71
  337.7 2.6 copy.8
  340.2 111.0 %reduce-scatter.17.cloned.1.call-done = bf16[1024,512]{0,1:T(8,128)(2,1)} async-done(((bf16[1024,8192]{0,1:T(8,128)(2,1)}), bf16[1024,512]{0,1:T(8,128)(2,1)}) %reduce-scatter.17.cloned.1.call-update) | async-done | bytes 1048592 | tf_op jit(solution)/shard_map/reduce_scatter | solution.py:74
  451.2 2.6 copy.9
  453.8 11.1 %reduce-scatter.9.cloned.1.call-done = bf16[128,1024]{1,0:T(8,128)(2,1)} async-done(((bf16[256,1024]{1,0:T(8,128)(2,1)}), bf16[128,1024]{1,0:T(8,128)(2,1)}) %reduce-scatter.9.cloned.1.call-update) | async-done | bytes 262160 | tf_op jit(solution)/shard_map/reduce_scatter | solution.py:49
  465.0 14.9 %reduce-scatter.13.cloned.1.call-done = bf16[128,1024]{1,0:T(8,128)(2,1)} async-done(((bf16[256,1024]{1,0:T(8,128)(2,1)}), bf16[128,1024]{1,0:T(8,128)(2,1)}) %reduce-scatter.13.cloned.1.call-update) | async-done | bytes 262160 | tf_op jit(solution)/shard_map/reduce_scatter | solution.py:65
Async XLA Ops:
  7.2 64.6 %reduce-scatter.11.cloned.1.call-start = ((), (), s32[]{:S(2)}) async-start(), calls=%async_computation.9 | async-start | bytes 5242880 | tf_op jit(solution)/shard_map/reduce_scatter | solution.py:57
  22.4 0.9 copy-start
  22.4 98.4 %reduce-scatter.7.cloned.1.call-start = ((), (), s32[]{:S(2)}) async-start(), calls=%async_computation.6 | async-start | bytes 5242880 | tf_op jit(solution)/shard_map/reduce_scatter | solution.py:40
  37.4 135.9 %all-gather.5.cloned.1.call-start = ((), (), s32[]{:S(2)}) async-start(), calls=%async_computation.10 | async-start | bytes 5242880 | tf_op jit(solution)/shard_map/all_gather | solution.py:63
  125.3 98.8 %all-gather.3.cloned.1.call-start = ((), (), s32[]{:S(2)}) async-start(), calls=%async_computation.7 | async-start | bytes 5242880 | tf_op jit(solution)/shard_map/all_gather | solution.py:47
  125.9 211.8 %reduce-scatter.15.cloned.1.call-start = ((), (), s32[]{:S(2)}) async-start(), calls=%async_computation.12 | async-start | bytes 17825792 | tf_op jit(solution)/shard_map/reduce_scatter | solution.py:71
  183.8 267.4 %reduce-scatter.17.cloned.1.call-start = ((), (), s32[]{:S(2)}) async-start(), calls=%async_computation.13 | async-start | bytes 17825792 | tf_op jit(solution)/shard_map/reduce_scatter | solution.py:74
  234.6 230.4 %reduce-scatter.9.cloned.1.call-start = ((), (), s32[]{:S(2)}) async-start(), calls=%async_computation.8 | async-start | bytes 786432 | tf_op jit(solution)/shard_map/reduce_scatter | solution.py:49
  248.0 231.8 %reduce-scatter.13.cloned.1.call-start = ((), (), s32[]{:S(2)}) async-start(), calls=%async_computation.11 | async-start | bytes 786432 | tf_op jit(solution)/shard_map/reduce_scatter | solution.py:65
Sparse Core Ops, SparseCore 0:
  22.6 49.1 reduce-scatter.10
  74.2 46.6 reduce-scatter.6
  125.4 47.8 all-gather.4
  175.4 48.5 all-gather.2
  227.3 110.2 reduce-scatter.14
  340.9 110.2 reduce-scatter.16
  454.2 10.7 reduce-scatter.8
  467.9 11.9 reduce-scatter.12
where the time goes:
time: 487 us
  waiting for transfers between devices  385 us (79%)
  matrix products  70.6 us (14%)
  between operations  14.1 us (3%)
  local copies, waits for them, and re-layouts  6.01 us (1%)
  blocking collectives  5.58 us (1%)
    reduce_scatter x1, waiting for transfers between devices, body(): lax.psum_scatter(down_local.astype(jnp.bfloat16), 'dp', scatter_dimension...  111 us
    reduce_scatter x1, waiting for transfers between devices, body(): lax.psum_scatter(up_local.astype(jnp.bfloat16), 'dp', scatter_dimension=1...  76.7 us
    reduce_scatter x1, waiting for transfers between devices, body(): lax.psum_scatter(rounded(jnp.dot(picked, w_up, preferred_element_type=jnp...  49.1 us
    all_gather x1, waiting for transfers between devices, body(): lax.all_gather((back * derivative).astype(jnp.bfloat16), 'row', axis=0, t...  47.4 us
    all_gather x1, waiting for transfers between devices, body(): lax.all_gather(activated.astype(jnp.bfloat16), 'row', axis=0, tiled=True)  40.2 us
    reduce_scatter x1, waiting for transfers between devices, body(): lax.psum_scatter(rounded(jnp.dot(picked, w_down, preferred_element_type=j...  34.3 us
    dot_general x2, matrix products, times_transposed(): lax.dot_general(left, right, (((1,), (1,)), ((), ())), preferred_element_...  26 us
    dot_general x2, matrix products, over_tokens(): lax.dot_general(left, right, (((0,), (0,)), ((), ())), preferred_element_...  21 us
  transfers between devices with their start and end apart: 8, of which 8 were waited for; matrix products, arithmetic and copies ran while one was open for 13% of the time, Pallas kernels for 0%

commit v1 on v0

v1 whole, which is shorter than its diff:
```python
import jax
import jax.numpy as jnp
from jax import lax
from jax.experimental import pallas as pl
from jax.experimental.pallas import tpu as pltpu
from jax.sharding import PartitionSpec as P

MESH = pl.DeviceIdType.MESH
bf16 = jnp.bfloat16
f32 = jnp.float32
gelu_coef = 0.7978845608
cubic_coef = 0.044715

SHARD = 128
WIDE = 1024
SLICE = 512
TOK = 16 * SHARD
HID = 2 * SLICE
CHUNKS = ((0, 256), (256, 256), (512, 512))


def mm(left, right, dim_left, dim_right):
    return lax.dot_general(
        left, right, (((dim_left,), (dim_right,)), ((), ())), preferred_element_type=f32
    )


def kernel(
    tok, cot, wup, wdn, oo, ga, gb,
    xv, wv, pb, pr, sb, sr, gv, ob, r1, r2, fb, gs,
    k_xin, k_x, k_ws, k_w, k_ag, k_bs, k_b, k_bs2, k_b2, k_ss, k_s, k_r1s, k_r1, k_r2s, k_r2, k_gs, k_g, k_os, k_o,
):
    dp, z, c = lax.axis_index("dp"), lax.axis_index("row"), lax.axis_index("col")
    y, x = lax.div(dp, 4), lax.rem(dp, 4)
    half, i = lax.div(z, 2), lax.rem(z, 2)
    za, zb = z + 1 - 2 * i, 3 - z
    tau = lax.rem(lax.div(z + 1, 2), 2)

    def remote(src, dst, send, recv, dev):
        return pltpu.make_async_remote_copy(
            src_ref=src, dst_ref=dst, send_sem=send, recv_sem=recv, device_id=dev, device_id_type=MESH
        )

    def arrived(dst, sem):
        pltpu.make_async_copy(dst, dst, sem).wait()

    def xy(o1, o2):
        px = lax.rem(x + o1 * (1 - c) + o2 * c, 4)
        py = lax.rem(y + o1 * c + o2 * (1 - c), 4)
        return px, py

    def dev(o1, o2):
        px, py = xy(o1, o2)
        return {"dp": py * 4 + px, "row": z, "col": c}

    def slot(o1, o2):
        px, py = xy(o1, o2)
        return lax.rem(px - py + 4, 4) * 4 + py

    def rows(s):
        return pl.ds(pl.multiple_of(s * SHARD, SHARD), SHARD)

    def at_z(zz, cc):
        return {"dp": dp, "row": zz, "col": cc}

    sends = []

    def put(local, src, dst, send, recv, to):
        copy = remote(src, dst, send, recv, to)
        if local is None:
            copy.start()
        else:
            @pl.when(local)
            def _():
                pltpu.make_async_copy(src, dst, recv).start()

            @pl.when(jnp.logical_not(local))
            def _():
                copy.start()
        sends.append((local, copy))

    barrier = pltpu.get_barrier_semaphore()
    peers = [at_z(za, 0), at_z(za, 1), at_z(zb, c), at_z(z, 1 - c)]
    peers += [dev(o, 0) for o in (1, 2, 3)] + [dev(0, o) for o in (1, 2, 3)]
    for peer in peers:
        pl.semaphore_signal(barrier, inc=1, device_id=peer, device_id_type=MESH)
    pl.semaphore_wait(barrier, len(peers))

    own = slot(0, 0)
    here = c == tau
    zx = z * (1 - lax.rem(c + tau, 2)) + za * lax.rem(c + tau, 2)
    for role, src in ((0, tok), (1, cot)):
        put(
            jnp.logical_and(here, c == role), src, xv.at[i, rows(own), :],
            k_xin.at[role], k_x.at[i, own], at_z(zx, role),
        )
    for k, (f0, fw) in enumerate(CHUNKS):
        n = fw // 2
        cols = pl.ds(pl.multiple_of(dp * SLICE + f0 // 2, 128), n)
        into = pl.ds(pl.multiple_of(f0 + c * n, 128), n)
        for rel, zz in ((1, za), (0, z)):
            for role, src in ((0, wup), (1, wdn)):
                put(
                    (c == role) if rel == 0 else None, src.at[:, cols], wv.at[i, :, into],
                    k_ws.at[k, rel, role], k_w.at[k, i, c], at_z(zz, role),
                )

    def weights(k):
        f0, fw = CHUNKS[k]
        n = fw // 2
        for db in range(2):
            for cc in range(2):
                arrived(wv.at[db, :, pl.ds(f0 + cc * n, n)], k_w.at[k, db, cc])

    count = [0]

    def shard_to(db, s, to):
        part = xv.at[db, rows(s), :]
        put(None, part, part, k_ag.at[count[0]], k_x.at[db, s], to)
        count[0] += 1

    def shard_in(db, s):
        arrived(xv.at[db, rows(s), :], k_x.at[db, s])

    def hidden(row0, m, f0, fw, step):
        r = pl.ds(row0, m)
        for n0 in range(f0, f0 + fw, step):
            cs = pl.ds(n0, step)
            part = mm(xv[0, r, :], wv[0, :, cs], 1, 0) + mm(xv[1, r, :], wv[1, :, cs], 1, 0)
            pb[r, cs] = part.astype(bf16)

    def hidden_line(o2, k):
        f0, fw = CHUNKS[k]

        @pl.loop(0, 4)
        def _(o1):
            hidden(pl.multiple_of(slot(o1, o2) * SHARD, SHARD), SHARD, f0, fw, fw)

        for o1 in range(4):
            s = slot(o1, o2)
            put(
                None, pb.at[rows(s), pl.ds(f0, fw)], pr.at[rows(s), pl.ds(f0, fw)],
                k_bs.at[k, s], k_b.at[k, s], at_z(zb, c),
            )

    def across(o1, from_):
        s = slot(o1, from_)
        for db in range(2):
            shard_in(db, s)
            if (from_, db) in ((3, 0), (1, 1)):
                shard_to(db, s, dev(0, 4 - from_))

    for db in range(2):
        shard_in(db, own)
        for to in (dev(1, 0), dev(3, 0), dev(0, 1), dev(0, 3)):
            shard_to(db, own, to)
    for o1 in (3, 1):
        s = slot(o1, 0)
        for db in range(2):
            shard_in(db, s)
            if (o1, db) in ((3, 0), (1, 1)):
                shard_to(db, s, dev(4 - o1, 0))
            for to in (dev(0, 1), dev(0, 3)):
                shard_to(db, s, to)
    across(0, 3)
    across(0, 1)
    for db in range(2):
        shard_in(db, slot(2, 0))
        for to in (dev(0, 1), dev(0, 3)):
            shard_to(db, slot(2, 0), to)
    weights(0)
    hidden_line(0, 0)
    for o1 in (3, 1):
        across(o1, 3)
        across(o1, 1)
    weights(1)
    hidden_line(0, 1)
    across(2, 3)
    across(2, 1)
    for o2 in (3, 1):
        hidden_line(o2, 0)
        hidden_line(o2, 1)
    for o1 in (0, 3, 1, 2):
        for db in range(2):
            shard_in(db, slot(o1, 2))
    hidden_line(2, 0)
    hidden_line(2, 1)
    weights(2)
    f2, w2 = CHUNKS[2]
    GROUP = 4 * SHARD
    for g in range(4):
        r = pl.ds(g * GROUP, GROUP)
        hidden(g * GROUP, GROUP, f2, w2, w2)
        put(None, pb.at[r, pl.ds(f2, w2)], pr.at[r, pl.ds(f2, w2)], k_bs2.at[g], k_b2.at[g], at_z(zb, c))

    def tiles(g, f0, body):
        @pl.loop(0, GROUP // 32)
        def _(a):
            for n0 in range(f0, f0 + SLICE, 256):
                body(pl.ds(pl.multiple_of(g * GROUP + a * 32, 32), 32), pl.ds(n0, 256))

    def combine(p, g):
        f0 = p * SLICE

        def body(r, cs):
            sb[r, cs] = (pb[r, cs].astype(f32) + pr[r, cs].astype(f32)).astype(bf16)

        tiles(g, f0, body)
        part = (pl.ds(g * GROUP, GROUP), pl.ds(f0, SLICE))
        put(None, sb.at[part], sr.at[part], k_ss.at[p, g], k_s.at[p, g], at_z(z, 1 - c))

    def activate(p, g):
        f0 = p * SLICE
        part = (pl.ds(g * GROUP, GROUP), pl.ds(f0, SLICE))
        arrived(sr.at[part], k_s.at[p, g])

        def grad(r, cs):
            hid, back = sb[r, cs].astype(f32), sr[r, cs].astype(f32)
            square = hid * hid
            t = jnp.tanh(gelu_coef * (hid + cubic_coef * square * hid))
            slope = 0.5 * (1.0 + t) + 0.5 * hid * (1.0 - t * t) * gelu_coef * (1.0 + 3.0 * cubic_coef * square)
            gv[r, cs] = (back * slope).astype(bf16)

        def act(r, cs):
            hid = sr[r, cs].astype(f32)
            t = jnp.tanh(gelu_coef * (hid + cubic_coef * hid * hid * hid))
            gv[r, cs] = (0.5 * hid * (1.0 + t)).astype(bf16)

        @pl.when(c == 0)
        def _():
            tiles(g, f0, grad)

        @pl.when(c == 1)
        def _():
            tiles(g, f0, act)

    def weight_grads(p):
        cs = pl.ds(p * SLICE, SLICE)

        @pl.loop(0, 2)
        def _(db):
            @pl.loop(0, WIDE // 256)
            def _(j):
                r = pl.ds(pl.multiple_of(j * 256, 256), 256)
                gs[db, r, cs] = mm(xv[db, :, r], gv[:, cs], 0, 0).astype(bf16)

        for k, (f0, fw) in enumerate(CHUNKS):
            if f0 // SLICE != p:
                continue
            n = fw // 2
            for rel, zz, db, out in ((1, za, 1 - i, gb), (0, z, i, ga)):
                for cc in range(2):
                    put(
                        (c == cc) if rel == 0 else None,
                        gs.at[db, :, pl.ds(f0 + cc * n, n)], out.at[c, :, pl.ds(f0 // 2, n)],
                        k_gs.at[k, rel, cc], k_g.at[k, rel, c], at_z(zz, cc),
                    )

    for g in range(4):
        for s in range(4 * g, 4 * g + 4):
            for k in range(2):
                f0, fw = CHUNKS[k]
                arrived(pr.at[rows(s), pl.ds(f0, fw)], k_b.at[k, s])
        combine(0, g)
        if g:
            activate(0, g - 1)
    activate(0, 3)
    weight_grads(0)

    def line_slot(g, o2):
        return 4 * g + lax.rem((1 - c) * (y + o2) + c * (x + o2 - g + 4), 4)

    def reduce_line(g):
        s = line_slot(g, 0)
        for o in range(3):
            arrived(r1.at[g, o], k_r1.at[g, o])

        @pl.loop(0, SHARD // 16)
        def _(a):
            src = pl.ds(pl.multiple_of(a * 16, 16), 16)
            dst = pl.ds(pl.multiple_of(s * SHARD + a * 16, 16), 16)
            for db in range(2):
                total = ob[db, dst, :].astype(f32)
                for o in range(3):
                    total = total + r1[g, o, db, src, :].astype(f32)
                ob[db, dst, :] = total.astype(bf16)

        o1 = lax.rem((1 - c) * (g + y - x + 4) + c * (x - g - y + 8), 4)
        slot2 = lax.rem(o1 + 3, 4)

        @pl.when(o1 != 0)
        def _():
            remote(
                ob.at[:, rows(s), :], r2.at[slot2], k_r2s.at[slot2], k_r2.at[slot2], dev(o1, 0)
            ).start()

    for g in range(4):
        r = pl.ds(g * GROUP, GROUP)
        arrived(pr.at[r, pl.ds(f2, w2)], k_b2.at[g])
        combine(1, g)
        activate(1, g)

        @pl.loop(0, 2)
        def _(db):
            @pl.loop(0, 2)
            def _(j):
                ds = pl.ds(pl.multiple_of(j * 512, 512), 512)
                ob[db, r, ds] = mm(gv[r, :], wv[db, ds, :], 1, 1).astype(bf16)

        for o in (2, 1, 3):
            s = line_slot(g, o)
            put(None, ob.at[:, rows(s), :], r1.at[g, o - 1], k_r1s.at[g, o - 1], k_r1.at[g, o - 1], dev(0, o))
        if g:
            reduce_line(g - 1)
    weight_grads(1)
    reduce_line(3)
    for o in range(3):
        arrived(r2.at[o], k_r2.at[o])

    @pl.loop(0, SHARD // 16)
    def _(a):
        src = pl.ds(pl.multiple_of(a * 16, 16), 16)
        dst = pl.ds(pl.multiple_of(own * SHARD + a * 16, 16), 16)
        for db in range(2):
            total = ob[db, dst, :].astype(f32)
            for o in range(3):
                total = total + r2[o, db, src, :].astype(f32)
            fb[db, src, :] = total.astype(bf16)

    for rel, zz, db in ((1, za, 1 - i), (0, z, i)):
        put(
            (tau == c) if rel == 0 else None, fb.at[db], oo.at[c], k_os.at[rel], k_o.at[c], at_z(zz, tau)
        )

    for role in range(2):
        arrived(oo.at[role], k_o.at[role])
        for k, (f0, fw) in enumerate(CHUNKS):
            for rel, out in ((0, ga), (1, gb)):
                arrived(out.at[role, :, pl.ds(f0 // 2, fw // 2)], k_g.at[k, rel, role])
    for o in range(3):
        remote(ob.at[:, pl.ds(0, SHARD), :], r2.at[o], k_r2s.at[o], k_r2.at[o], dev(1, 0)).wait_send()
    for local, copy in sends:
        if local is None:
            copy.wait_send()
        else:
            @pl.when(jnp.logical_not(local))
            def _():
                copy.wait_send()


def body(tokens, w_up, w_down, cotangent):
    batch_total = tokens.shape[0] * lax.axis_size("col") * lax.axis_size("dp")
    grad_scale = float(batch_total) ** (-0.5)
    dma = pltpu.SemaphoreType.DMA
    anywhere = pl.BlockSpec(memory_space=pl.ANY)
    oo, ga, gb = pl.pallas_call(
        kernel,
        out_shape=(
            jax.ShapeDtypeStruct((2, SHARD, WIDE), bf16),
            jax.ShapeDtypeStruct((2, WIDE, SLICE), bf16),
            jax.ShapeDtypeStruct((2, WIDE, SLICE), bf16),
        ),
        in_specs=[anywhere] * 4,
        out_specs=(anywhere,) * 3,
        scratch_shapes=[
            pltpu.VMEM((2, TOK, WIDE), bf16),
            pltpu.VMEM((2, WIDE, HID), bf16),
            pltpu.VMEM((TOK, HID), bf16),
            pltpu.VMEM((TOK, HID), bf16),
            pltpu.VMEM((TOK, HID), bf16),
            pltpu.VMEM((TOK, HID), bf16),
            pltpu.VMEM((TOK, HID), bf16),
            pltpu.VMEM((2, TOK, WIDE), bf16),
            pltpu.VMEM((4, 3, 2, SHARD, WIDE), bf16),
            pltpu.VMEM((3, 2, SHARD, WIDE), bf16),
            pltpu.VMEM((2, SHARD, WIDE), bf16),
            pltpu.VMEM((2, WIDE, HID), bf16),
            dma((2,)), dma((2, 16)),
            dma((3, 2, 2)), dma((3, 2, 2)),
            dma((30,)),
            dma((2, 16)), dma((2, 16)), dma((4,)), dma((4,)),
            dma((2, 4)), dma((2, 4)),
            dma((4, 3)), dma((4, 3)), dma((3,)), dma((3,)),
            dma((3, 2, 2)), dma((3, 2, 2)),
            dma((2,)), dma((2,)),
        ],
        compiler_params=pltpu.CompilerParams(
            collective_id=0, has_side_effects=True, vmem_limit_bytes=63 << 20
        ),
        name="ffn",
    )(tokens, cotangent, w_up, w_down)
    up_grad = grad_scale * (ga[0].astype(f32) + gb[0].astype(f32))
    down_grad = grad_scale * (ga[1].astype(f32) + gb[1].astype(f32))
    return (oo[1], oo[0], up_grad, down_grad)


def solution(mesh):
    placed = (P(("dp", "col"), "row"), P("row", "col"), P("row", "col"), P(("dp", "col"), "row"))
    return jax.shard_map(
        body,
        mesh=mesh,
        in_specs=placed,
        out_specs=(
            P(("dp", "col"), "row"),
            P(("dp", "col"), "row"),
            P("row", ("col", "dp")),
            P("row", ("col", "dp")),
        ),
        check_vma=False,
    )
```

time: 487 us -> 204 us (0.42)
  waiting for transfers between devices: 385 us -> 0 us
  Pallas kernels: 0 us -> 195 us
  matrix products: 70.6 us -> 0 us
  between operations: 14.1 us -> 0.64 us
  blocking collectives: 5.58 us -> 0 us
    reduce_scatter x6 -> x0, waiting for transfers between devices: 297 us -> none  [the longest x1 111 us: body(): lax.psum_scatter(down_local.astype(jnp.bfloat16), 'dp', scatter_dimension...]
    pallas_call x0 -> x1, Pallas kernels: none -> 195 us  [body(): pl.pallas_call(kernel, out_shape=(jax.ShapeDtypeStruct((2, SHARD, WIDE),...]
    all_gather x2 -> x0, waiting for transfers between devices: 87.6 us -> none  [the longest x1 47.4 us: body(): lax.all_gather((back * derivative).astype(jnp.bfloat16), 'row', axis=0, t...]
    dot_general x6 -> x0, matrix products: 70.6 us -> none  [the longest x2 26 us: times_transposed(): lax.dot_general(left, right, (((1,), (1,)), ((), ())), preferred_element_...]
    unnamed x4 -> x0, local copies, waits for them, and re-layouts: 6.01 us -> none
    all_gather x2 -> x0, blocking collectives: 5.58 us -> none  [the longest x1 3.4 us: body(): grad_block = lax.all_gather(cotangent, 'col', axis=0, tiled=True)]
    mul x0 -> x1, other arithmetic: none -> 4.88 us  [body(): down_grad = grad_scale * (ga[1].astype(f32) + gb[1].astype(f32))]
  transfers between devices with their start and end apart: 8 -> 0, of which waited for: 8 -> 0; matrix products, arithmetic and copies ran while one was open for 13% -> 0% of each run, Pallas kernels for 0% -> 0%
where the time goes in v1:
time: 204 us; the launch traced here: 202 us
  Pallas kernels  195 us (96%)
  other arithmetic  4.88 us (2%)
    pallas_call x1, Pallas kernels, body(): pl.pallas_call(kernel, out_shape=(jax.ShapeDtypeStruct((2, SHARD, WIDE),...  195 us
    mul x1, other arithmetic, body(): down_grad = grad_scale * (ga[1].astype(f32) + gb[1].astype(f32))  4.88 us

profile of v1, /device:TPU:1, one launch (start us, length us, event | category | flops | bytes accessed | tf_op | source)
XLA Modules:
  0.0 202.4 jit_solution(7490761176094558411)
XLA Ops:
  0.6 195.0 %ffn.1 = (bf16[2,128,1024]{2,1,0:T(8,128)(2,1)}, bf16[2,1024,512]{2,1,0:T(8,128)(2,1)}, bf16[2,1024,512]{2,1,0:T(8,128)(2,1)}) custom-call(bf16[128,1024]{1,0:T(8,128)(2,1)} %tok.1, bf16[128,1024]{1,0:T(8,128)(2,1)} %cot.1, bf16[1024,8192]{1,0:T(8,128)(2,1)} %wup.1, bf16[1024,8192]{1,0:T(8,128)(2,1)} %wdn.1), custom_call_target="tpu_custom_call" | custom-call | tf_op jit(solution)/shard_map/ffn/pallas_call | solution.py:356
  195.7 1.9 slice_bitcast_fusion
  197.5 4.9 %multiply_bitcast_fusion = (f32[1024,512]{1,0:T(8,128)}, f32[1024,512]{1,0:T(8,128)}) fusion(bf16[2,1024,512]{2,1,0:T(8,128)(2,1)} %get-tuple-element.9, bf16[2,1024,512]{2,1,0:T(8,128)(2,1)} %get-tuple-element.8), kind=kLoop, calls=%fused_computation | loop fusion | flops 4194304 | bytes 8388608 | tf_op jit(solution)/shard_map/mul | solution.py:393

commit v2 on v0

v2 whole, which is shorter than its diff:
```python
import jax
import jax.numpy as jnp
from jax import lax
from jax.experimental import pallas as pl
from jax.experimental.pallas import tpu as pltpu
from jax.sharding import PartitionSpec as P

MESH = pl.DeviceIdType.MESH
bf16 = jnp.bfloat16
f32 = jnp.float32
gelu_coef = 0.7978845608
cubic_coef = 0.044715

SHARD = 128
WIDE = 1024
SLICE = 512
TOK = 16 * SHARD
HID = 2 * SLICE
UNIT = 128
CHUNKS = ((0, 2), (2, 2), (4, 1), (5, 3))
EARLY = 5 * UNIT
PASSES = ((0, EARLY), (EARLY, HID - EARLY))
PIECE = SHARD // 4
GROUP = 16 * PIECE


def mm(left, right, dim_left, dim_right):
    return lax.dot_general(
        left, right, (((dim_left,), (dim_right,)), ((), ())), preferred_element_type=f32
    )


def kernel(
    tok, cot, wup, wdn, oo, ga, gb,
    xv, wv, pb, pr, sb, sr, gv, ob, r1, rl, r2, fb, gs, acc,
    k_xin, k_x, k_ws, k_w, k_ag, k_bs, k_b, k_bs2, k_b2, k_ss, k_s,
    k_r1s, k_r1, k_rls, k_rl, k_r2s, k_r2, k_gs, k_g, k_os, k_o,
):
    dp, z, c = lax.axis_index("dp"), lax.axis_index("row"), lax.axis_index("col")
    y, x = lax.div(dp, 4), lax.rem(dp, 4)
    half, i = lax.div(z, 2), lax.rem(z, 2)
    za, zb = z + 1 - 2 * i, 3 - z
    tau = lax.rem(lax.div(z + 1, 2), 2)

    def remote(src, dst, send, recv, dev):
        return pltpu.make_async_remote_copy(
            src_ref=src, dst_ref=dst, send_sem=send, recv_sem=recv, device_id=dev, device_id_type=MESH
        )

    def arrived(dst, sem):
        pltpu.make_async_copy(dst, dst, sem).wait()

    a1, a2 = x * (1 - c) + y * c, y * (1 - c) + x * c

    def place(o1, o2):
        return lax.rem(a2 + o2, 4), lax.rem(a1 + o1, 4)

    def number(p):
        return p[0] * 4 + p[1]

    def dev(o1, o2):
        p2, p1 = place(o1, o2)
        return {"dp": (p1 * c + p2 * (1 - c)) * 4 + p1 * (1 - c) + p2 * c, "row": z, "col": c}

    def at_z(zz, cc):
        return {"dp": dp, "row": zz, "col": cc}

    sends = []

    def put(local, src, dst, send, recv, to):
        copy = remote(src, dst, send, recv, to)
        if local is None:
            copy.start()
        else:
            @pl.when(local)
            def _():
                pltpu.make_async_copy(src, dst, recv).start()

            @pl.when(jnp.logical_not(local))
            def _():
                copy.start()
        sends.append((local, copy))

    barrier = pltpu.get_barrier_semaphore()
    peers = [at_z(za, 0), at_z(za, 1), at_z(zb, c), at_z(z, 1 - c)]
    peers += [dev(o, 0) for o in (1, 2, 3)] + [dev(0, o) for o in (1, 2, 3)]
    for peer in peers:
        pl.semaphore_signal(barrier, inc=1, device_id=peer, device_id_type=MESH)
    pl.semaphore_wait(barrier, len(peers))

    own = place(0, 0)
    here = c == tau
    zx = z * (1 - lax.rem(c + tau, 2)) + za * lax.rem(c + tau, 2)
    for role, src, p in ((0, tok, (y, x)), (1, cot, (x, y))):
        put(
            jnp.logical_and(here, c == role), src, xv.at[i, :, p[0], p[1]],
            k_xin.at[role], k_x.at[i, number(p)], at_z(zx, role),
        )
    for m in range(4):
        u = 2 * m + c
        cols = pl.ds(pl.multiple_of(dp * SLICE + m * UNIT, UNIT), UNIT)
        into = pl.ds(pl.multiple_of(u * UNIT, UNIT), UNIT)
        for rel, zz in ((1, za), (0, z)):
            for role, src in ((0, wup), (1, wdn)):
                put(
                    (c == role) if rel == 0 else None, src.at[:, cols], wv.at[i, :, into],
                    k_ws.at[m, rel, role], k_w.at[u, i], at_z(zz, role),
                )

    def weights(k):
        u0, n = CHUNKS[k]
        for u in range(u0, u0 + n):
            for db in range(2):
                arrived(wv.at[db, :, pl.ds(u * UNIT, UNIT)], k_w.at[u, db])

    count = [0]

    def shard_to(db, p, to):
        part = xv.at[db, :, p[0], p[1]]
        put(None, part, part, k_ag.at[count[0]], k_x.at[db, number(p)], to)
        count[0] += 1

    def shard_in(db, p):
        arrived(xv.at[db, :, p[0], p[1]], k_x.at[db, number(p)])

    def hidden(part, m, shape, f0, fw):
        cs = pl.ds(f0, fw)
        total = [mm(xv[(db, *part)].reshape(m, WIDE), wv[db, :, cs], 1, 0) for db in range(2)]
        pb[(*part, slice(None), cs)] = (total[0] + total[1]).astype(bf16).reshape(*shape, PIECE, fw)

    def hidden_line(o1, o2s, chunks):
        for k in chunks:
            f0, fw = CHUNKS[k][0] * UNIT, CHUNKS[k][1] * UNIT

            @pl.loop(0, len(o2s))
            def _(j):
                p = place(o1, lax.rem(j + o2s[0], 4))
                hidden((slice(None), p[0], p[1]), SHARD, (4,), f0, fw)

            for o2 in o2s:
                p = place(o1, o2)
                at = (slice(None), p[0], p[1], slice(None), pl.ds(f0, fw))
                put(None, pb.at[at], pr.at[at], k_bs.at[k, number(p)], k_b.at[k, number(p)], at_z(zb, c))

    halves = (i, 1 - i)

    def across(o1, o2):
        p = place(o1, o2)
        for way, db in enumerate(halves):
            shard_in(db, p)
            if (o2, way) in ((3, 0), (1, 1)):
                shard_to(db, p, dev(0, 4 - o2))

    near, far, full = (3, 0, 1), (2,), (3, 0, 1, 2)
    for db in halves:
        shard_in(db, own)
        for to in (dev(1, 0), dev(3, 0), dev(0, 1), dev(0, 3)):
            shard_to(db, own, to)
    for o1 in (3, 1):
        p = place(o1, 0)
        for way, db in enumerate(halves):
            shard_in(db, p)
            if (o1, way) in ((3, 0), (1, 1)):
                shard_to(db, p, dev(4 - o1, 0))
            for to in (dev(0, 1), dev(0, 3)):
                shard_to(db, p, to)
    across(0, 3)
    across(0, 1)
    for db in halves:
        shard_in(db, place(2, 0))
        for to in (dev(0, 1), dev(0, 3)):
            shard_to(db, place(2, 0), to)
    weights(0)
    hidden_line(0, near, (0,))
    across(3, 3)
    across(3, 1)
    hidden_line(3, near, (0,))
    across(0, 2)
    hidden_line(0, far, (0,))
    weights(1)
    hidden_line(0, full, (1,))
    hidden_line(3, near, (1,))
    across(1, 3)
    across(1, 1)
    hidden_line(1, near, (0, 1))
    across(3, 2)
    hidden_line(3, far, (0, 1))
    weights(2)
    hidden_line(0, full, (2,))
    hidden_line(3, full, (2,))
    hidden_line(1, near, (2,))
    across(2, 3)
    across(2, 1)
    hidden_line(2, near, (0, 1, 2))
    across(1, 2)
    hidden_line(1, far, (0, 1, 2))
    across(2, 2)
    hidden_line(2, far, (0, 1, 2))
    weights(3)
    f2, w2 = PASSES[1]

    def late(g):
        return (g, slice(None), slice(None), slice(None), pl.ds(f2, w2))

    for g in range(4):
        hidden((g, slice(None), slice(None)), GROUP, (4, 4), f2, w2)
        put(None, pb.at[late(g)], pr.at[late(g)], k_bs2.at[g], k_b2.at[g], at_z(zb, c))

    def tiles(g, p, body):
        f0, fw = PASSES[p]

        @pl.loop(0, 4)
        def _(t2):
            @pl.loop(0, 4)
            def _(t1):
                for n0 in range(f0, f0 + fw, UNIT):
                    body((g, t2, t1, slice(None), pl.ds(n0, UNIT)))

    def combine(p, g):
        def body(at):
            sb[at] = (pb[at].astype(f32) + pr[at].astype(f32)).astype(bf16)

        tiles(g, p, body)
        for j in range(4):
            cs = pl.ds(*PASSES[p])
            put(
                None, sb.at[g, :, j, :, cs], sr.at[g, j, :, :, cs],
                k_ss.at[p, g, j], k_s.at[p, g, j], at_z(z, 1 - c),
            )

    def activate(p, g):
        for j in range(4):
            arrived(sr.at[g, j, :, :, pl.ds(*PASSES[p])], k_s.at[p, g, j])

        def grad(at):
            hid, back = sb[at].astype(f32), sr[at].astype(f32)
            square = hid * hid
            t = jnp.tanh(gelu_coef * (hid + cubic_coef * square * hid))
            slope = 0.5 * (1.0 + t) + 0.5 * hid * (1.0 - t * t) * gelu_coef * (1.0 + 3.0 * cubic_coef * square)
            gv[at] = (back * slope).astype(bf16)

        def act(at):
            hid = sr[at].astype(f32)
            t = jnp.tanh(gelu_coef * (hid + cubic_coef * hid * hid * hid))
            gv[at] = (0.5 * hid * (1.0 + t)).astype(bf16)

        @pl.when(c == 0)
        def _():
            tiles(g, p, grad)

        @pl.when(c == 1)
        def _():
            tiles(g, p, act)

    def grads_out(p, rel, part):
        zz, db, out = ((z, i, ga), (za, 1 - i, gb))[rel]
        r = pl.ds(part * 512, 512)
        for u in range(PASSES[p][0] // UNIT, sum(PASSES[p]) // UNIT):
            m, cc = u // 2, u % 2
            put(
                (c == cc) if rel == 0 else None,
                gs.at[db, r, pl.ds(u * UNIT, UNIT)], out.at[c, r, pl.ds(m * UNIT, UNIT)],
                k_gs.at[u, rel, part], k_g.at[m, rel, c, part], at_z(zz, cc),
            )

    def weight_grads(g):
        f0, fw = PASSES[0 if g is None else 1]
        cs = pl.ds(f0, fw)
        t, n = (slice(None), TOK) if g is None else (g, GROUP)
        for rel, db in ((1, 1 - i), (0, i)):
            for part in range(2):

                @pl.loop(0, 2)
                def _(j):
                    r = pl.ds(pl.multiple_of(part * 512 + j * 256, 256), 256)
                    total = mm(xv[db, t, :, :, :, r].reshape(n, 256), gv[t, :, :, :, cs].reshape(n, fw), 0, 0)
                    if g:
                        total = total + acc[db, r, :]
                    if g is None or g == 3:
                        gs[db, r, cs] = total.astype(bf16)
                    else:
                        acc[db, r, :] = total

                if g is None:
                    grads_out(0, rel, part)
                elif g == 3:
                    grads_out(1, rel, part)

    for k in range(3):
        for p2 in range(4):
            for p1 in range(4):
                at = (slice(None), p2, p1, slice(None), pl.ds(CHUNKS[k][0] * UNIT, CHUNKS[k][1] * UNIT))
                arrived(pr.at[at], k_b.at[k, p2 * 4 + p1])
    for g in range(4):
        combine(0, g)
        if g:
            activate(0, g - 1)
    activate(0, 3)
    weight_grads(None)

    def add_to(target, others):
        @pl.loop(0, 4)
        def _(t1):
            total = target[t1].astype(f32)
            for other in others:
                total = total + other[t1].astype(f32)
            target[t1] = total.astype(bf16)

    def line(g, o2, db):
        return ob.at[db, g, lax.rem(a2 + o2, 4)]

    def to_line(g, o2, db, side):
        put(
            None, line(g, o2, db), r1.at[g, side, db],
            k_r1s.at[g, side, db], k_r1.at[g, side, db], dev(0, o2),
        )

    def reduce_start(g):
        put(None, line(g, 2, 0), rl.at[g, 0], k_rls.at[g, 0], k_rl.at[g, 0], dev(0, 1))
        put(None, line(g, 2, 1), rl.at[g, 1], k_rls.at[g, 1], k_rl.at[g, 1], dev(0, 3))
        to_line(g, 1, 1, 0)
        to_line(g, 3, 0, 1)

    def reduce_relay(g):
        for db, o2 in ((0, 1), (1, 3)):
            arrived(rl.at[g, db], k_rl.at[g, db])
            add_to(line(g, o2, db), [rl.at[g, db]])
            to_line(g, o2, db, db)

    def reduce_line(g):
        for db in range(2):
            for side in range(2):
                arrived(r1.at[g, side, db], k_r1.at[g, side, db])
            add_to(line(g, 0, db), [r1.at[g, 0, db], r1.at[g, 1, db]])
        for o1 in (2, 1, 3):
            put(
                None, ob.at[:, g, a2, lax.rem(a1 + o1, 4)], r2.at[g, o1 - 1],
                k_r2s.at[g, o1 - 1], k_r2.at[g, o1 - 1], dev(o1, 0),
            )

    def finish(g):
        for o in range(3):
            arrived(r2.at[g, o], k_r2.at[g, o])
        for db in range(2):
            total = ob[db, g, a2, a1].astype(f32)
            for o in range(3):
                total = total + r2[g, o, db].astype(f32)
            fb[g, db] = total.astype(bf16)
        for rel, zz, db in ((1, za, 1 - i), (0, z, i)):
            put(
                (tau == c) if rel == 0 else None, fb.at[g, db], oo.at[c, g],
                k_os.at[g, rel], k_o.at[g, c], at_z(zz, tau),
            )

    for g in range(4):
        arrived(pr.at[late(g)], k_b2.at[g])
        combine(1, g)
        if g:
            weight_grads(g - 1)
            reduce_relay(g - 1)
        if g > 1:
            reduce_line(g - 2)
        activate(1, g)

        @pl.loop(0, 2)
        def _(db):
            @pl.loop(0, 2)
            def _(j):
                ds = pl.ds(pl.multiple_of(j * 512, 512), 512)
                prod = mm(gv[g].reshape(GROUP, HID), wv[db, ds, :], 1, 1)
                ob[db, g, :, :, :, ds] = prod.astype(bf16).reshape(4, 4, PIECE, 512)

        reduce_start(g)
    weight_grads(3)
    reduce_relay(3)
    finish(0)
    reduce_line(2)
    finish(1)
    reduce_line(3)
    finish(2)
    finish(3)

    for role in range(2):
        for g in range(4):
            arrived(oo.at[role, g], k_o.at[g, role])
        for m in range(4):
            for rel, out in ((0, ga), (1, gb)):
                for part in range(2):
                    arrived(
                        out.at[role, pl.ds(part * 512, 512), pl.ds(m * UNIT, UNIT)], k_g.at[m, rel, role, part]
                    )
    for local, copy in sends:
        if local is None:
            copy.wait_send()
        else:
            @pl.when(jnp.logical_not(local))
            def _():
                copy.wait_send()


def body(tokens, w_up, w_down, cotangent):
    batch_total = tokens.shape[0] * lax.axis_size("col") * lax.axis_size("dp")
    grad_scale = float(batch_total) ** (-0.5)
    dma = pltpu.SemaphoreType.DMA
    anywhere = pl.BlockSpec(memory_space=pl.ANY)
    oo, ga, gb = pl.pallas_call(
        kernel,
        out_shape=(
            jax.ShapeDtypeStruct((2, 4, PIECE, WIDE), bf16),
            jax.ShapeDtypeStruct((2, WIDE, SLICE), bf16),
            jax.ShapeDtypeStruct((2, WIDE, SLICE), bf16),
        ),
        in_specs=[anywhere] * 4,
        out_specs=(anywhere,) * 3,
        scratch_shapes=[
            pltpu.VMEM((2, 4, 4, 4, PIECE, WIDE), bf16),
            pltpu.VMEM((2, WIDE, HID), bf16),
            pltpu.VMEM((4, 4, 4, PIECE, HID), bf16),
            pltpu.VMEM((4, 4, 4, PIECE, HID), bf16),
            pltpu.VMEM((4, 4, 4, PIECE, HID), bf16),
            pltpu.VMEM((4, 4, 4, PIECE, HID), bf16),
            pltpu.VMEM((4, 4, 4, PIECE, HID), bf16),
            pltpu.VMEM((2, 4, 4, 4, PIECE, WIDE), bf16),
            pltpu.VMEM((4, 2, 2, 4, PIECE, WIDE), bf16),
            pltpu.VMEM((4, 2, 4, PIECE, WIDE), bf16),
            pltpu.VMEM((4, 3, 2, PIECE, WIDE), bf16),
            pltpu.VMEM((4, 2, PIECE, WIDE), bf16),
            pltpu.VMEM((2, WIDE, HID), bf16),
            pltpu.VMEM((2, WIDE, PASSES[1][1]), f32),
            dma((2,)), dma((2, 16)),
            dma((4, 2, 2)), dma((8, 2)),
            dma((30,)),
            dma((3, 16)), dma((3, 16)), dma((4,)), dma((4,)),
            dma((2, 4, 4)), dma((2, 4, 4)),
            dma((4, 2, 2)), dma((4, 2, 2)), dma((4, 2)), dma((4, 2)),
            dma((4, 3)), dma((4, 3)),
            dma((8, 2, 2)), dma((4, 2, 2, 2)),
            dma((4, 2)), dma((4, 2)),
        ],
        compiler_params=pltpu.CompilerParams(
            collective_id=0, has_side_effects=True, vmem_limit_bytes=63 << 20
        ),
        name="ffn",
    )(tokens.reshape(4, PIECE, WIDE), cotangent.reshape(4, PIECE, WIDE), w_up, w_down)
    oo = oo.reshape(2, SHARD, WIDE)
    up_grad = grad_scale * (ga[0].astype(f32) + gb[0].astype(f32))
    down_grad = grad_scale * (ga[1].astype(f32) + gb[1].astype(f32))
    return (oo[1], oo[0], up_grad, down_grad)


def solution(mesh):
    placed = (P(("dp", "col"), "row"), P("row", "col"), P("row", "col"), P(("dp", "col"), "row"))
    return jax.shard_map(
        body,
        mesh=mesh,
        in_specs=placed,
        out_specs=(
            P(("dp", "col"), "row"),
            P(("dp", "col"), "row"),
            P("row", ("col", "dp")),
            P("row", ("col", "dp")),
        ),
        check_vma=False,
    )
```

time: 487 us -> 185 us (0.38)
  waiting for transfers between devices: 385 us -> 0 us
  Pallas kernels: 0 us -> 176 us
  matrix products: 70.6 us -> 0 us
  between operations: 14.1 us -> 0.64 us
  blocking collectives: 5.58 us -> 0 us
    reduce_scatter x6 -> x0, waiting for transfers between devices: 297 us -> none  [the longest x1 111 us: body(): lax.psum_scatter(down_local.astype(jnp.bfloat16), 'dp', scatter_dimension...]
    pallas_call x0 -> x1, Pallas kernels: none -> 176 us  [body(): pl.pallas_call(kernel, out_shape=(jax.ShapeDtypeStruct((2, 4, PIECE, WIDE...]
    all_gather x2 -> x0, waiting for transfers between devices: 87.6 us -> none  [the longest x1 47.4 us: body(): lax.all_gather((back * derivative).astype(jnp.bfloat16), 'row', axis=0, t...]
    dot_general x6 -> x0, matrix products: 70.6 us -> none  [the longest x2 26 us: times_transposed(): lax.dot_general(left, right, (((1,), (1,)), ((), ())), preferred_element_...]
    unnamed x4 -> x0, local copies, waits for them, and re-layouts: 6.01 us -> none
    all_gather x2 -> x0, blocking collectives: 5.58 us -> none  [the longest x1 3.4 us: body(): grad_block = lax.all_gather(cotangent, 'col', axis=0, tiled=True)]
    mul x0 -> x1, other arithmetic: none -> 4.88 us  [body(): down_grad = grad_scale * (ga[1].astype(f32) + gb[1].astype(f32))]
  transfers between devices with their start and end apart: 8 -> 0, of which waited for: 8 -> 0; matrix products, arithmetic and copies ran while one was open for 13% -> 0% of each run, Pallas kernels for 0% -> 0%
where the time goes in v2:
time: 185 us; the launch traced here: 183 us
  Pallas kernels  176 us (95%)
  other arithmetic  4.88 us (3%)
  local copies, waits for them, and re-layouts  1.85 us (1%)
    pallas_call x1, Pallas kernels, body(): pl.pallas_call(kernel, out_shape=(jax.ShapeDtypeStruct((2, 4, PIECE, WIDE...  176 us
    mul x1, other arithmetic, body(): down_grad = grad_scale * (ga[1].astype(f32) + gb[1].astype(f32))  4.88 us

profile of v2, /device:TPU:1, one launch (start us, length us, event | category | flops | bytes accessed | tf_op | source)
XLA Modules:
  0.0 183.4 jit_solution(5175693496168517754)
XLA Ops:
  0.6 176.0 %ffn.1 = (bf16[2,4,32,1024]{3,2,1,0:T(8,128)(2,1)}, bf16[2,1024,512]{2,1,0:T(8,128)(2,1)}, bf16[2,1024,512]{2,1,0:T(8,128)(2,1)}) custom-call(bf16[4,32,1024]{2,1,0:T(8,128)(2,1)} %bitcast.8, bf16[4,32,1024]{2,1,0:T(8,128)(2,1)} %bitcast.9, bf16[1024,8192]{1,0:T(8,128)(2,1)} %wup.1, bf16[1024,8192]{1,0:T(8,128)(2,1)} %wdn.1), custom_call_target="tpu_custom_call" | custom-call | tf_op jit(solution)/shard_map/ffn/pallas_call | solution.py:406
  176.7 1.9 %fusion = (bf16[1,4,32,1024]{3,2,1,0:T(8,128)(2,1)}, bf16[1,4,32,1024]{3,2,1,0:T(8,128)(2,1)}) fusion(bf16[2,4,32,1024]{3,2,1,0:T(8,128)(2,1)} %get-tuple-element.7), kind=kLoop, calls=%fused_computation.2 | loop fusion | bytes 1048576 | tf_op jit(solution)/shard_map/slice | solution.py:448
  178.5 4.9 %multiply_bitcast_fusion = (f32[1024,512]{1,0:T(8,128)}, f32[1024,512]{1,0:T(8,128)}) fusion(bf16[2,1024,512]{2,1,0:T(8,128)(2,1)} %get-tuple-element.9, bf16[2,1024,512]{2,1,0:T(8,128)(2,1)} %get-tuple-element.8), kind=kLoop, calls=%fused_computation | loop fusion | flops 4194304 | bytes 8388608 | tf_op jit(solution)/shard_map/mul | solution.py:447

commit v3 on v2

--- a/solution.py
+++ b/solution.py
@@ -17,8 +17,8 @@
 TOK = 16 * SHARD
 HID = 2 * SLICE
 UNIT = 128
-CHUNKS = ((0, 2), (2, 2), (4, 1), (5, 3))
-EARLY = 5 * UNIT
+CHUNKS = ((0, 2), (2, 1), (3, 1), (4, 4))
+EARLY = 4 * UNIT
 PASSES = ((0, EARLY), (EARLY, HID - EARLY))
 PIECE = SHARD // 4
 GROUP = 16 * PIECE
@@ -33,7 +33,7 @@
 def kernel(
     tok, cot, wup, wdn, oo, ga, gb,
     xv, wv, pb, pr, sb, sr, gv, ob, r1, rl, r2, fb, gs, acc,
-    k_xin, k_x, k_ws, k_w, k_ag, k_bs, k_b, k_bs2, k_b2, k_ss, k_s,
+    k_xin, k_x, k_ws, k_w, k_ag, k_bs, k_b, k_bs2, k_b2, k_ss, k_s, k_ts, k_t,
     k_r1s, k_r1, k_rls, k_rl, k_r2s, k_r2, k_gs, k_g, k_os, k_o,
 ):
     dp, z, c = lax.axis_index("dp"), lax.axis_index("row"), lax.axis_index("col")
@@ -128,19 +128,25 @@
         total = [mm(xv[(db, *part)].reshape(m, WIDE), wv[db, :, cs], 1, 0) for db in range(2)]
         pb[(*part, slice(None), cs)] = (total[0] + total[1]).astype(bf16).reshape(*shape, PIECE, fw)
 
-    def hidden_line(o1, o2s, chunks):
-        for k in chunks:
-            f0, fw = CHUNKS[k][0] * UNIT, CHUNKS[k][1] * UNIT
-
-            @pl.loop(0, len(o2s))
-            def _(j):
-                p = place(o1, lax.rem(j + o2s[0], 4))
-                hidden((slice(None), p[0], p[1]), SHARD, (4,), f0, fw)
-
-            for o2 in o2s:
-                p = place(o1, o2)
-                at = (slice(None), p[0], p[1], slice(None), pl.ds(f0, fw))
-                put(None, pb.at[at], pr.at[at], k_bs.at[k, number(p)], k_b.at[k, number(p)], at_z(zb, c))
+    expected = {}
+
+    def hidden_set(shards, first, last):
+        n, offsets = shards
+        u0, u1 = CHUNKS[first][0], sum(CHUNKS[last])
+        f0, fw = u0 * UNIT, (u1 - u0) * UNIT
+
+        @pl.loop(0, n)
+        def _(j):
+            p = place(*offsets(j))
+            hidden((slice(None), p[0], p[1]), SHARD, (4,), f0, fw)
+
+        for j in range(n):
+            o = offsets(j)
+            p = place(*o)
+            at = (slice(None), p[0], p[1], slice(None), pl.ds(f0, fw))
+            sem = k_b.at[first, number(p)]
+            put(None, pb.at[at], pr.at[at], k_bs.at[first, number(p)], sem, at_z(zb, c))
+            expected.setdefault(o, []).append((at, sem))
 
     halves = (i, 1 - i)
 
@@ -151,7 +157,10 @@
             if (o2, way) in ((3, 0), (1, 1)):
                 shard_to(db, p, dev(0, 4 - o2))
 
-    near, far, full = (3, 0, 1), (2,), (3, 0, 1, 2)
+    centre, beside = (3, lambda j: (0, (j + 3) % 4)), (3, lambda j: (j + 1, 0))
+    low, high, across_far = (2, lambda j: (3, 3 - 2 * j)), (2, lambda j: (1, 3 - 2 * j)), (1, lambda j: (0, 2))
+    edge = (2, lambda j: (2, 3 - 2 * j))
+    corners = [(1, lambda j, o1=o1: (o1, 2)) for o1 in (3, 1, 2)]
     for db in halves:
         shard_in(db, own)
         for to in (dev(1, 0), dev(3, 0), dev(0, 1), dev(0, 3)):
@@ -171,31 +180,28 @@
         for to in (dev(0, 1), dev(0, 3)):
             shard_to(db, place(2, 0), to)
     weights(0)
-    hidden_line(0, near, (0,))
+    hidden_set(centre, 0, 0)
+    hidden_set(beside, 0, 0)
     across(3, 3)
     across(3, 1)
-    hidden_line(3, near, (0,))
-    across(0, 2)
-    hidden_line(0, far, (0,))
+    hidden_set(low, 0, 0)
     weights(1)
-    hidden_line(0, full, (1,))
-    hidden_line(3, near, (1,))
+    for shards in (centre, beside, low):
+        hidden_set(shards, 1, 1)
     across(1, 3)
     across(1, 1)
-    hidden_line(1, near, (0, 1))
-    across(3, 2)
-    hidden_line(3, far, (0, 1))
+    hidden_set(high, 0, 1)
+    across(0, 2)
+    hidden_set(across_far, 0, 1)
     weights(2)
-    hidden_line(0, full, (2,))
-    hidden_line(3, full, (2,))
-    hidden_line(1, near, (2,))
+    for shards in (centre, beside, low, high, across_far):
+        hidden_set(shards, 2, 2)
     across(2, 3)
     across(2, 1)
-    hidden_line(2, near, (0, 1, 2))
-    across(1, 2)
-    hidden_line(1, far, (0, 1, 2))
-    across(2, 2)
-    hidden_line(2, far, (0, 1, 2))
+    hidden_set(edge, 0, 2)
+    for shards in corners:
+        across(*shards[1](0))
+        hidden_set(shards, 0, 2)
     weights(3)
     f2, w2 = PASSES[1]
 
@@ -206,51 +212,85 @@
         hidden((g, slice(None), slice(None)), GROUP, (4, 4), f2, w2)
         put(None, pb.at[late(g)], pr.at[late(g)], k_bs2.at[g], k_b2.at[g], at_z(zb, c))
 
-    def tiles(g, p, body):
+    def columns(p, body):
         f0, fw = PASSES[p]
-
+        for n0 in range(f0, f0 + fw, UNIT):
+            body(pl.ds(n0, UNIT))
+
+    def over_set(shards, body):
+        @pl.loop(0, shards[0])
+        def _(j):
+            p2, p1 = place(*shards[1](j))
+
+            @pl.loop(0, 4)
+            def _(g):
+                columns(0, lambda cs: body((g, p2, p1, slice(None), cs)))
+
+    def over_group(g, body):
         @pl.loop(0, 4)
-        def _(t2):
+        def _(p2):
             @pl.loop(0, 4)
-            def _(t1):
-                for n0 in range(f0, f0 + fw, UNIT):
-                    body((g, t2, t1, slice(None), pl.ds(n0, UNIT)))
-
-    def combine(p, g):
-        def body(at):
-            sb[at] = (pb[at].astype(f32) + pr[at].astype(f32)).astype(bf16)
-
-        tiles(g, p, body)
+            def _(p1):
+                columns(1, lambda cs: body((g, p2, p1, slice(None), cs)))
+
+    def add_pair(at):
+        sb[at] = (pb[at].astype(f32) + pr[at].astype(f32)).astype(bf16)
+
+    def grad(at):
+        hid, back = sb[at].astype(f32), sr[at].astype(f32)
+        square = hid * hid
+        t = jnp.tanh(gelu_coef * (hid + cubic_coef * square * hid))
+        slope = 0.5 * (1.0 + t) + 0.5 * hid * (1.0 - t * t) * gelu_coef * (1.0 + 3.0 * cubic_coef * square)
+        gv[at] = (back * slope).astype(bf16)
+
+    def act(at):
+        hid = sr[at].astype(f32)
+        t = jnp.tanh(gelu_coef * (hid + cubic_coef * hid * hid * hid))
+        gv[at] = (0.5 * hid * (1.0 + t)).astype(bf16)
+
+    def combine_set(shards):
+        cs = pl.ds(*PASSES[0])
+        places = [shards[1](j) for j in range(shards[0])]
+        for o in places:
+            for at, sem in expected[o]:
+                arrived(pr.at[at], sem)
+        over_set(shards, add_pair)
+        for o in places:
+            p2, p1 = place(*o)
+            put(
+                None, sb.at[:, p2, p1, :, cs], sr.at[:, p1, p2, :, cs],
+                k_ss.at[p2 * 4 + p1], k_s.at[p1 * 4 + p2], at_z(z, 1 - c),
+            )
+
+    def activate_sets(sets):
+        for shards in sets:
+            for j in range(shards[0]):
+                p2, p1 = place(*shards[1](j))
+                arrived(sr.at[:, p2, p1, :, pl.ds(*PASSES[0])], k_s.at[p2 * 4 + p1])
+        for role, body in ((0, grad), (1, act)):
+
+            @pl.when(c == role)
+            def _():
+                for shards in sets:
+                    over_set(shards, body)
+
+    def combine(g):
+        over_group(g, add_pair)
         for j in range(4):
-            cs = pl.ds(*PASSES[p])
+            cs = pl.ds(*PASSES[1])
             put(
                 None, sb.at[g, :, j, :, cs], sr.at[g, j, :, :, cs],
-                k_ss.at[p, g, j], k_s.at[p, g, j], at_z(z, 1 - c),
+                k_ts.at[g, j], k_t.at[g, j], at_z(z, 1 - c),
             )
 
-    def activate(p, g):
+    def activate(g):
         for j in range(4):
-            arrived(sr.at[g, j, :, :, pl.ds(*PASSES[p])], k_s.at[p, g, j])
-
-        def grad(at):
-            hid, back = sb[at].astype(f32), sr[at].astype(f32)
-            square = hid * hid
-            t = jnp.tanh(gelu_coef * (hid + cubic_coef * square * hid))
-            slope = 0.5 * (1.0 + t) + 0.5 * hid * (1.0 - t * t) * gelu_coef * (1.0 + 3.0 * cubic_coef * square)
-            gv[at] = (back * slope).astype(bf16)
-
-        def act(at):
-            hid = sr[at].astype(f32)
-            t = jnp.tanh(gelu_coef * (hid + cubic_coef * hid * hid * hid))
-            gv[at] = (0.5 * hid * (1.0 + t)).astype(bf16)
-
-        @pl.when(c == 0)
-        def _():
-            tiles(g, p, grad)
-
-        @pl.when(c == 1)
-        def _():
-            tiles(g, p, act)
+            arrived(sr.at[g, j, :, :, pl.ds(*PASSES[1])], k_t.at[g, j])
+        for role, body in ((0, grad), (1, act)):
+
+            @pl.when(c == role)
+            def _():
+                over_group(g, body)
 
     def grads_out(p, rel, part):
         zz, db, out = ((z, i, ga), (za, 1 - i, gb))[rel]
@@ -263,11 +303,12 @@
                 k_gs.at[u, rel, part], k_g.at[m, rel, c, part], at_z(zz, cc),
             )
 
-    def weight_grads(g):
+    def weight_grads(g, rels=(1, 0)):
         f0, fw = PASSES[0 if g is None else 1]
         cs = pl.ds(f0, fw)
         t, n = (slice(None), TOK) if g is None else (g, GROUP)
-        for rel, db in ((1, 1 - i), (0, i)):
+        for rel in rels:
+            db = (i, 1 - i)[rel]
             for part in range(2):
 
                 @pl.loop(0, 2)
@@ -286,17 +327,13 @@
                 elif g == 3:
                     grads_out(1, rel, part)
 
-    for k in range(3):
-        for p2 in range(4):
-            for p1 in range(4):
-                at = (slice(None), p2, p1, slice(None), pl.ds(CHUNKS[k][0] * UNIT, CHUNKS[k][1] * UNIT))
-                arrived(pr.at[at], k_b.at[k, p2 * 4 + p1])
-    for g in range(4):
-        combine(0, g)
-        if g:
-            activate(0, g - 1)
-    activate(0, 3)
-    weight_grads(None)
+    for shards in (centre, beside, low, high, across_far):
+        combine_set(shards)
+    block = (9, lambda j: ((j % 3 + 3) % 4, (j // 3 + 3) % 4))
+    activate_sets([block, (2, lambda j: (2 * j, 2 - 2 * j))])
+    for shards in (edge, *corners):
+        combine_set(shards)
+    activate_sets([edge, (3, lambda j: ((j + 1) % 4, 2))])
 
     def add_to(target, others):
         @pl.loop(0, 4)
@@ -352,16 +389,7 @@
                 k_os.at[g, rel], k_o.at[g, c], at_z(zz, tau),
             )
 
-    for g in range(4):
-        arrived(pr.at[late(g)], k_b2.at[g])
-        combine(1, g)
-        if g:
-            weight_grads(g - 1)
-            reduce_relay(g - 1)
-        if g > 1:
-            reduce_line(g - 2)
-        activate(1, g)
-
+    def out(g):
         @pl.loop(0, 2)
         def _(db):
             @pl.loop(0, 2)
@@ -370,8 +398,24 @@
                 prod = mm(gv[g].reshape(GROUP, HID), wv[db, ds, :], 1, 1)
                 ob[db, g, :, :, :, ds] = prod.astype(bf16).reshape(4, 4, PIECE, 512)
 
+    for g in range(4):
+        if g == 0:
+            weight_grads(None, (1,))
+        arrived(pr.at[late(g)], k_b2.at[g])
+        combine(g)
+        if g == 0:
+            weight_grads(None, (0,))
+        else:
+            weight_grads(g - 1)
+            reduce_relay(g - 1)
+        if g > 1:
+            reduce_line(g - 2)
+        activate(g)
+        if g == 3:
+            weight_grads(3, (1,))
+        out(g)
         reduce_start(g)
-    weight_grads(3)
+    weight_grads(3, (0,))
     reduce_relay(3)
     finish(0)
     reduce_line(2)
@@ -431,7 +475,7 @@
             dma((4, 2, 2)), dma((8, 2)),
             dma((30,)),
             dma((3, 16)), dma((3, 16)), dma((4,)), dma((4,)),
-            dma((2, 4, 4)), dma((2, 4, 4)),
+            dma((16,)), dma((16,)), dma((4, 4)), dma((4, 4)),
             dma((4, 2, 2)), dma((4, 2, 2)), dma((4, 2)), dma((4, 2)),
             dma((4, 3)), dma((4, 3)),
             dma((8, 2, 2)), dma((4, 2, 2, 2)),

time: 185 us -> 173 us (0.935)
  Pallas kernels: 176 us -> 165 us
    pallas_call x1, Pallas kernels: 176 us -> 165 us  [body(): pl.pallas_call(kernel, out_shape=(jax.ShapeDtypeStruct((2, 4, PIECE, WIDE...]
where the time goes in v3:
time: 173 us
  Pallas kernels  165 us (95%)
  other arithmetic  4.88 us (3%)
  local copies, waits for them, and re-layouts  1.85 us (1%)
    pallas_call x1, Pallas kernels, body(): pl.pallas_call(kernel, out_shape=(jax.ShapeDtypeStruct((2, 4, PIECE, WIDE...  165 us
    mul x1, other arithmetic, body(): down_grad = grad_scale * (ga[1].astype(f32) + gb[1].astype(f32))  4.88 us

profile of v3, /device:TPU:1, one launch (start us, length us, event | category | flops | bytes accessed | tf_op | source)
XLA Modules:
  0.0 172.8 jit_solution(4607941383831490522)
XLA Ops:
  0.6 165.4 %ffn.1 = (bf16[2,4,32,1024]{3,2,1,0:T(8,128)(2,1)}, bf16[2,1024,512]{2,1,0:T(8,128)(2,1)}, bf16[2,1024,512]{2,1,0:T(8,128)(2,1)}) custom-call(bf16[4,32,1024]{2,1,0:T(8,128)(2,1)} %bitcast.8, bf16[4,32,1024]{2,1,0:T(8,128)(2,1)} %bitcast.9, bf16[1024,8192]{1,0:T(8,128)(2,1)} %wup.1, bf16[1024,8192]{1,0:T(8,128)(2,1)} %wdn.1), custom_call_target="tpu_custom_call" | custom-call | tf_op jit(solution)/shard_map/ffn/pallas_call | solution.py:450
  166.0 1.9 %fusion = (bf16[1,4,32,1024]{3,2,1,0:T(8,128)(2,1)}, bf16[1,4,32,1024]{3,2,1,0:T(8,128)(2,1)}) fusion(bf16[2,4,32,1024]{3,2,1,0:T(8,128)(2,1)} %get-tuple-element.7), kind=kLoop, calls=%fused_computation.2 | loop fusion | bytes 1048576 | tf_op jit(solution)/shard_map/slice | solution.py:492
  167.9 4.9 %multiply_bitcast_fusion = (f32[1024,512]{1,0:T(8,128)}, f32[1024,512]{1,0:T(8,128)}) fusion(bf16[2,1024,512]{2,1,0:T(8,128)(2,1)} %get-tuple-element.9, bf16[2,1024,512]{2,1,0:T(8,128)(2,1)} %get-tuple-element.8), kind=kLoop, calls=%fused_computation | loop fusion | flops 4194304 | bytes 8388608 | tf_op jit(solution)/shard_map/mul | solution.py:491

commit v4 on v3

--- a/solution.py
+++ b/solution.py
@@ -1,3 +1,5 @@
+import functools
+
 import jax
 import jax.numpy as jnp
 from jax import lax
@@ -17,7 +19,7 @@
 TOK = 16 * SHARD
 HID = 2 * SLICE
 UNIT = 128
-CHUNKS = ((0, 2), (2, 1), (3, 1), (4, 4))
+CHUNKS = ((0, 2), (2, 2), (4, 4))
 EARLY = 4 * UNIT
 PASSES = ((0, EARLY), (EARLY, HID - EARLY))
 PIECE = SHARD // 4
@@ -193,16 +195,13 @@
     hidden_set(high, 0, 1)
     across(0, 2)
     hidden_set(across_far, 0, 1)
-    weights(2)
-    for shards in (centre, beside, low, high, across_far):
-        hidden_set(shards, 2, 2)
     across(2, 3)
     across(2, 1)
-    hidden_set(edge, 0, 2)
+    hidden_set(edge, 0, 1)
     for shards in corners:
         across(*shards[1](0))
-        hidden_set(shards, 0, 2)
-    weights(3)
+        hidden_set(shards, 0, 1)
+    weights(2)
     f2, w2 = PASSES[1]
 
     def late(g):
@@ -440,6 +439,13 @@
             @pl.when(jnp.logical_not(local))
             def _():
                 copy.wait_send()
+
+
+def finish_kernel(scale, oo, ga, gb, out, ig, up, down):
+    ig[...] = oo[0]
+    out[...] = oo[1]
+    up[...] = scale * (ga[0].astype(f32) + gb[0].astype(f32))
+    down[...] = scale * (ga[1].astype(f32) + gb[1].astype(f32))
 
 
 def body(tokens, w_up, w_down, cotangent):
@@ -474,7 +480,7 @@
             dma((2,)), dma((2, 16)),
             dma((4, 2, 2)), dma((8, 2)),
             dma((30,)),
-            dma((3, 16)), dma((3, 16)), dma((4,)), dma((4,)),
+            dma((2, 16)), dma((2, 16)), dma((4,)), dma((4,)),
             dma((16,)), dma((16,)), dma((4, 4)), dma((4, 4)),
             dma((4, 2, 2)), dma((4, 2, 2)), dma((4, 2)), dma((4, 2)),
             dma((4, 3)), dma((4, 3)),
@@ -487,9 +493,20 @@
         name="ffn",
     )(tokens.reshape(4, PIECE, WIDE), cotangent.reshape(4, PIECE, WIDE), w_up, w_down)
     oo = oo.reshape(2, SHARD, WIDE)
-    up_grad = grad_scale * (ga[0].astype(f32) + gb[0].astype(f32))
-    down_grad = grad_scale * (ga[1].astype(f32) + gb[1].astype(f32))
-    return (oo[1], oo[0], up_grad, down_grad)
+    steps = 4
+    rows, wide = WIDE // steps, SHARD // steps
+    small, large = pl.BlockSpec((wide, WIDE), lambda k: (k, 0)), pl.BlockSpec((rows, SLICE), lambda k: (k, 0))
+    pair = pl.BlockSpec((2, rows, SLICE), lambda k: (0, k, 0))
+    token_out = jax.ShapeDtypeStruct((SHARD, WIDE), bf16)
+    weight_out = jax.ShapeDtypeStruct((WIDE, SLICE), f32)
+    return pl.pallas_call(
+        functools.partial(finish_kernel, grad_scale),
+        grid=(steps,),
+        out_shape=(token_out, token_out, weight_out, weight_out),
+        in_specs=[pl.BlockSpec((2, wide, WIDE), lambda k: (0, k, 0)), pair, pair],
+        out_specs=(small, small, large, large),
+        name="finish",
+    )(oo, ga, gb)
 
 
 def solution(mesh):

time: 173 us -> 170 us (0.983)
  other arithmetic: 4.88 us -> 0 us
  Pallas kernels: 165 us -> 169 us
  local copies, waits for them, and re-layouts: 1.85 us -> 0 us
    pallas_call x0 -> x1, Pallas kernels: none -> 5 us  [body(): pl.pallas_call(functools.partial(finish_kernel, grad_scale), grid=(steps,...]
    mul x1 -> x0, other arithmetic: 4.88 us -> none  [body(): down_grad = grad_scale * (ga[1].astype(f32) + gb[1].astype(f32))]
    slice x1 -> x0, local copies, waits for them, and re-layouts: 1.85 us -> none  [body(): return (oo[1], oo[0], up_grad, down_grad)]
where the time goes in v4:
time: 170 us
  Pallas kernels  169 us (99%)
    pallas_call x1, Pallas kernels, body(): pl.pallas_call(kernel, out_shape=(jax.ShapeDtypeStruct((2, 4, PIECE, WIDE...  164 us
    pallas_call x1, Pallas kernels, body(): pl.pallas_call(functools.partial(finish_kernel, grad_scale), grid=(steps,...  5 us

profile of v4, /device:TPU:1, one launch (start us, length us, event | category | flops | bytes accessed | tf_op | source)
XLA Modules:
  0.0 169.5 jit_solution(17909952711069706049)
XLA Ops:
  0.6 163.9 %ffn.1 = (bf16[2,4,32,1024]{3,2,1,0:T(8,128)(2,1)}, bf16[2,1024,512]{2,1,0:T(8,128)(2,1)}, bf16[2,1024,512]{2,1,0:T(8,128)(2,1)}) custom-call(bf16[4,32,1024]{2,1,0:T(8,128)(2,1)} %bitcast.4, bf16[4,32,1024]{2,1,0:T(8,128)(2,1)} %bitcast.5, bf16[1024,8192]{1,0:T(8,128)(2,1)} %wup.1, bf16[1024,8192]{1,0:T(8,128)(2,1)} %wdn.1), custom_call_target="tpu_custom_call" | custom-call | tf_op jit(solution)/shard_map/ffn/pallas_call | solution.py:456
  164.5 5.0 %finish.1 = (bf16[128,1024]{1,0:T(8,128)(2,1)}, bf16[128,1024]{1,0:T(8,128)(2,1)}, f32[1024,512]{1,0:T(8,128)}, f32[1024,512]{1,0:T(8,128)}) custom-call(bf16[2,128,1024]{2,1,0:T(8,128)(2,1)} %bitcast.3, bf16[2,1024,512]{2,1,0:T(8,128)(2,1)} %get-tuple-element.8.ga, bf16[2,1024,512]{2,1,0:T(8,128)(2,1)} %get-tuple-element.9.gb), custom_call_target="tpu_custom_call" | custom-call | tf_op jit(solution)/shard_map/finish/pallas_call | solution.py:502

commit v5 on v4

--- a/solution.py
+++ b/solution.py
@@ -400,12 +400,13 @@
     for g in range(4):
         if g == 0:
             weight_grads(None, (1,))
+        else:
+            weight_grads(g - 1)
         arrived(pr.at[late(g)], k_b2.at[g])
         combine(g)
         if g == 0:
             weight_grads(None, (0,))
         else:
-            weight_grads(g - 1)
             reduce_relay(g - 1)
         if g > 1:
             reduce_line(g - 2)
@@ -493,7 +494,7 @@
         name="ffn",
     )(tokens.reshape(4, PIECE, WIDE), cotangent.reshape(4, PIECE, WIDE), w_up, w_down)
     oo = oo.reshape(2, SHARD, WIDE)
-    steps = 4
+    steps = 2
     rows, wide = WIDE // steps, SHARD // steps
     small, large = pl.BlockSpec((wide, WIDE), lambda k: (k, 0)), pl.BlockSpec((rows, SLICE), lambda k: (k, 0))
     pair = pl.BlockSpec((2, rows, SLICE), lambda k: (0, k, 0))

time: 170 us -> 168 us (0.988)
  Pallas kernels: 169 us -> 165 us
    pallas_call x1, Pallas kernels: 164 us -> 161 us  [body(): pl.pallas_call(kernel, out_shape=(jax.ShapeDtypeStruct((2, 4, PIECE, WIDE...]
where the time goes in v5:
time: 168 us; the launch traced here: 166 us
  Pallas kernels  165 us (98%)
    pallas_call x1, Pallas kernels, body(): pl.pallas_call(kernel, out_shape=(jax.ShapeDtypeStruct((2, 4, PIECE, WIDE...  161 us
    pallas_call x1, Pallas kernels, body(): pl.pallas_call(functools.partial(finish_kernel, grad_scale), grid=(steps,...  4.01 us

profile of v5, /device:TPU:1, one launch (start us, length us, event | category | flops | bytes accessed | tf_op | source)
XLA Modules:
  0.0 166.1 jit_solution(18118352037621248372)
XLA Ops:
  0.6 161.5 %ffn.1 = (bf16[2,4,32,1024]{3,2,1,0:T(8,128)(2,1)}, bf16[2,1024,512]{2,1,0:T(8,128)(2,1)}, bf16[2,1024,512]{2,1,0:T(8,128)(2,1)}) custom-call(bf16[4,32,1024]{2,1,0:T(8,128)(2,1)} %bitcast.4, bf16[4,32,1024]{2,1,0:T(8,128)(2,1)} %bitcast.5, bf16[1024,8192]{1,0:T(8,128)(2,1)} %wup.1, bf16[1024,8192]{1,0:T(8,128)(2,1)} %wdn.1), custom_call_target="tpu_custom_call" | custom-call | tf_op jit(solution)/shard_map/ffn/pallas_call | solution.py:457
  162.1 4.0 %finish.1 = (bf16[128,1024]{1,0:T(8,128)(2,1)}, bf16[128,1024]{1,0:T(8,128)(2,1)}, f32[1024,512]{1,0:T(8,128)}, f32[1024,512]{1,0:T(8,128)}) custom-call(bf16[2,128,1024]{2,1,0:T(8,128)(2,1)} %bitcast.3, bf16[2,1024,512]{2,1,0:T(8,128)(2,1)} %get-tuple-element.8.ga, bf16[2,1024,512]{2,1,0:T(8,128)(2,1)} %get-tuple-element.9.gb), custom_call_target="tpu_custom_call" | custom-call | tf_op jit(solution)/shard_map/finish/pallas_call | solution.py:503
